TPU v7x, 512 devices: a whole 4x8x8 slice. The times are simulated.
512 devices in a mesh: seq: 64 (over y, z), mp: 8 (over x, core).
Axes of the slice: x: 4, y: 8, z: 8, core: 2. Of those that a mesh axis runs over, the one named last changes fastest.
Arguments:
- patch_states: bfloat16 [32768, 2048], P('seq'), may hold values from -6 to 6
- mlp_gain: bfloat16 [2048], replicated, may hold values from 0.099609375 to 1.8984375
- up_weight: bfloat16 [2048, 7168], P('seq', 'mp')
- down_weight: bfloat16 [7168, 2048], P('mp', 'seq')
- kv_gain: bfloat16 [2048], replicated, may hold values from 0.099609375 to 1.8984375
- kv_weight: bfloat16 [2048, 2048], P(None, 'mp'), may hold values from -0.125 to 0.125
- byte_states: bfloat16 [65536, 1024], P('seq'), may hold values from -6 to 6
- query_weight: bfloat16 [1024, 1024], P(None, 'mp'), may hold values from -0.1875 to 0.1875
- out_weight: bfloat16 [1024, 1024], P('mp'), may hold values from -0.75 to 0.75
- patch_counts: int32 [64], P('seq'), may hold values from 256 to 512, as said below
- byte_patch: int32 [65536], P('seq'), may hold values from 0 to 511, as said below
Outputs:
- decoded: bfloat16 [65536, 1024], P(('seq', 'mp'))
Inputs may be any that keep to these rules, and one draw needn't show every extreme that they name: `patch_counts`: exactly 512 in some block and exactly 256 in another, in every draw. `byte_patch`: within each seq block of 1024 bytes the values start at 0, never fall, rise by at most one from one byte to the next, and end at that block's patch count minus one.
All inputs are finite; a program needn't handle non-finite values.
Results may differ from a plain program's by a relative error of at most 0.02.
Values may be sent and summed in bfloat16 or wider, within the bound.
No kernel may reach another device: no remote copies, remote signals or barrier semaphores. Data moves between devices by JAX's collectives and lax.ppermute only.
A program may use at most 64 MiB of HBM per device.

v0:
```python
import math
import jax
import jax.numpy as jnp
from jax import lax
from jax.sharding import PartitionSpec as P

HS = 128
WIN = 1024


def entering(value, axis, join, neutral):
    count, mine = (lax.axis_size(axis), lax.axis_index(axis))
    pieces = jax.tree.map(lambda part: lax.all_gather(part, axis), value)
    so_far = jax.tree.map(
        lambda part, zero: jnp.full_like(part, 0) + jnp.asarray(zero, part.dtype), value, neutral
    )

    def step(position, so_far):
        longer = join(so_far, jax.tree.map(lambda part: part[position], pieces))
        return jax.tree.map(lambda new, old: jnp.where(position < mine, new, old), longer, so_far)

    return lax.fori_loop(0, count - 1, step, so_far)


def from_behind(value, axis, steps):
    count = lax.axis_size(axis)
    leading, last = (max(0, -steps), min(count, count - steps))
    return lax.ppermute(value, axis, [(source, source + steps) for source in range(leading, last)])


def scale_rows(values, gain):
    return values * lax.rsqrt(jnp.mean(values * values, axis=-1, keepdims=True) + 1e-05) * gain


def unit_rows(values):
    return values * lax.rsqrt(jnp.mean(values * values, axis=-1, keepdims=True) + 1e-06)


def on_device(
    patch_states,
    mlp_gain,
    up_weight,
    down_weight,
    kv_gain,
    kv_weight,
    byte_states,
    query_weight,
    out_weight,
    patch_counts,
    byte_patch,
):
    patch_rows = patch_states.shape[0]
    normed = scale_rows(patch_states.astype(jnp.float32), mlp_gain.astype(jnp.float32)).astype(
        jnp.bfloat16
    )
    preact = jnp.dot(
        normed,
        lax.all_gather(up_weight, "seq", axis=0, tiled=True),
        preferred_element_type=jnp.float32,
    )
    hidden = jax.nn.gelu(preact, approximate=False).astype(jnp.bfloat16)
    kv_scale = kv_gain.astype(jnp.float32)
    partial_value = jnp.dot(
        hidden,
        lax.all_gather(down_weight, "seq", axis=1, tiled=True),
        preferred_element_type=jnp.float32,
    )
    mixed_out = lax.psum(partial_value.astype(jnp.bfloat16), "mp").astype(jnp.float32)
    kv_in = scale_rows(patch_states.astype(jnp.float32) + mixed_out, kv_scale).astype(jnp.bfloat16)
    heads_here = kv_weight.shape[1] // (2 * HS)
    projected = jnp.dot(kv_in, kv_weight, preferred_element_type=jnp.float32).reshape(
        patch_rows, heads_here, 2, HS
    )
    keys = unit_rows(projected[:, :, 0])
    kv_pack = (
        jnp.stack([keys, projected[:, :, 1]], axis=2)
        .astype(jnp.bfloat16)
        .reshape(patch_rows, heads_here * 2 * HS)
    )
    bytes_here = byte_states.shape[0]
    query_proj = jnp.dot(byte_states, query_weight, preferred_element_type=jnp.float32).reshape(
        bytes_here, heads_here, HS
    )
    queries = unit_rows(query_proj).astype(jnp.bfloat16)
    depth_back = (WIN + patch_rows // 2 - 2) // (patch_rows // 2)
    own_count = patch_counts[0]
    slots = jnp.arange(depth_back, dtype=jnp.int32)

    def join_windows(earlier_part, later_part):
        early_vals, early_len = earlier_part
        late_vals, late_len = later_part
        from_late = slots >= depth_back - late_len
        wanted = slots + late_len
        early_pick = jnp.sum(
            jnp.where(slots[None, :] == wanted[:, None], early_vals[None, :], 0), axis=1
        ).astype(jnp.int32)
        joined = jnp.where(from_late, late_vals, early_pick).astype(jnp.int32)
        return (joined, jnp.minimum(early_len + late_len, depth_back).astype(jnp.int32))

    own_window = jnp.where(slots == depth_back - 1, own_count, 0)
    empty_window = (jnp.zeros((depth_back,), jnp.int32), jnp.zeros((), jnp.int32))
    prior_counts, prior_len = entering(
        (own_window, jnp.ones((), jnp.int32)), "seq", join_windows, empty_window
    )
    earlier = []
    forwarded = kv_pack
    for offset_back in range(1, depth_back + 1):
        forwarded = from_behind(forwarded, "seq", 1)
        earlier.append(forwarded)
    score_scale = 2.0 / math.sqrt(HS)
    positions = jnp.arange(patch_rows, dtype=jnp.int32)
    numerator = jnp.zeros((bytes_here, heads_here, HS), jnp.float32)
    denominator = jnp.zeros((heads_here, bytes_here), jnp.float32)
    for distance, kv_block in enumerate([kv_pack] + earlier):
        if distance == 0:
            first_id = jnp.zeros((), jnp.int32)
            live_count = own_count
        else:
            first_id = -jnp.sum(prior_counts[depth_back - distance :]).astype(jnp.int32)
            live_count = prior_counts[depth_back - distance]
        key_ids = first_id + positions
        usable = (
            (positions < live_count)[None, :]
            & (key_ids[None, :] <= byte_patch[:, None])
            & (key_ids[None, :] > byte_patch[:, None] - WIN)
        )
        kv_parts = kv_block.reshape(patch_rows, heads_here, 2, HS)
        scores = (
            jnp.einsum(
                "bhd,phd->hbp", queries, kv_parts[:, :, 0], preferred_element_type=jnp.float32
            )
            * score_scale
        )
        weights = jnp.where(usable[None], jnp.exp(scores), 0.0)
        numerator = numerator + jnp.einsum(
            "hbp,phd->bhd",
            weights.astype(jnp.bfloat16),
            kv_parts[:, :, 1],
            preferred_element_type=jnp.float32,
        )
        denominator = denominator + jnp.sum(weights, axis=-1)
    attended = (
        (numerator / jnp.transpose(denominator)[:, :, None])
        .astype(jnp.bfloat16)
        .reshape(bytes_here, heads_here * HS)
    )
    decoded = lax.psum_scatter(
        jnp.dot(attended, out_weight, preferred_element_type=jnp.float32).astype(jnp.bfloat16),
        "mp",
        scatter_dimension=0,
        tiled=True,
    )
    return decoded


def solution(mesh):
    in_specs = (
        P("seq", None),
        P(),
        P("seq", "mp"),
        P("mp", "seq"),
        P(),
        P(None, "mp"),
        P("seq", None),
        P(None, "mp"),
        P("mp", None),
        P("seq"),
        P("seq"),
    )
    out_specs = P(("seq", "mp"), None)
    return jax.shard_map(
        on_device, mesh=mesh, in_specs=in_specs, out_specs=out_specs, check_vma=False
    )
```

profile of v0, /device:TPU:8, one launch (start us, length us, event | category | flops | bytes accessed | tf_op | source)
XLA Modules:
  0.0 416.1 jit_solution(15715362171986909808)
XLA Ops:
  6.5 0.7 all-gather.4.cloned.1.call-update
  7.3 0.7 all-gather.6.cloned.1.call-update
  8.7 48.6 %all-gather = s32[64,1,4]{2,1,0:T(1,128)S(1)} all-gather(s32[1,1,4]{2,1,0:T(1,128)S(1)} %fusion.71), channel_id=1, replica_groups=mesh['seq'=64,'mp'=8] {'seq'}, dimensions={0}, use_global_device_ids=true | all-gather | bytes 1040 | tf_op jit(solution)/shard_map/all_gather | solution.py:13
  57.3 1.3 dynamic-slice
  58.7 0.8 dynamic-update-slice
  59.5 23.7 %all-reduce = s32[64]{0:T(128)S(1)} all-reduce(s32[64]{0:T(128)S(1)} %dynamic-update-slice), channel_id=1, replica_groups=mesh['seq'=64,'mp'=8] {'seq'}, use_global_device_ids=true, to_apply=%add | all-reduce | flops 64 | bytes 512
  83.2 130.9 %while.15 = (s32[]{:T(128)}, s32[4]{0:T(128)S(1)}, s32[]{:T(128)}, s32[64]{0:T(128)S(1)}, s32[64,4]{1,0:T(8,128)S(1)}, /*index=5*/s32[]{:T(128)}, s32[]{:T(128)}, s32[]{:T(128)}) while((s32[]{:T(128)}, s32[4]{0:T(128)S(1)}, s32[]{:T(128)}, s32[64]{0:T(128)S(1)}, s32[64,4]{1,0:T(8,128)S(1)}, /*index=5*/s32[]{:T(128)}, ...), condition=%wide.region_7.8_spmd.clone.clone, body=%wide.region_5.7_spmd.clone.clone.sunk | while | flops 69 | bytes 301 | solution.py:22
  85.3 0.6 dynamic_slice.22
  87.4 0.6 dynamic_slice.22
  91.5 0.6 dynamic_slice.22
  95.7 0.6 dynamic_slice.22
  97.8 0.6 dynamic_slice.22
  101.9 0.6 dynamic_slice.22
  106.1 0.6 dynamic_slice.22
  108.1 0.6 dynamic_slice.22
  110.2 0.6 dynamic_slice.22
  112.3 0.6 dynamic_slice.22
  116.5 0.6 dynamic_slice.22
  214.1 0.7 convert_element_type.71
  214.8 0.7 convert_element_type.76
  215.5 0.7 reduce_sum.131
  216.2 0.7 fusion.102
  218.1 0.8 slice_reduce_fusion
  219.6 0.8 slice_reduce_fusion.1
  221.0 0.7 iota_compare_fusion.6
  221.7 0.7 iota_compare_fusion.3
  223.6 2.1 fusion.2
  225.8 13.4 %convolution_convert_fusion = bf16[512,2048]{1,0:T(8,128)(2,1)} fusion(bf16[896,2048]{0,1:T(8,128)(2,1)} %all-gather.6.cloned.1.call-done, bf16[2048,896]{1,0:T(8,128)(2,1)} %all-gather.4.cloned.1.call-done, bf16[512,2048]{1,0:T(8,128)(2,1)} %param.13, f32[2048]{0:T(1024)S(1)} %convert_element_type.71, f32[512]{0:T(512)S(1)} %add_rsqrt_fusion.3), kind=kOutput, calls=%fused_computation.15 | convolution fusion | flops 3793158144 | bytes 11544576 | tf_op jit(solution)/shard_map/dot_general | solution.py:63
  239.3 0.8 copy-done.4
  240.1 0.8 multiply_reduce_fusion.1
  241.1 70.2 %all-reduce.3.cloned.1.call-done = bf16[512,2048]{1,0:T(8,128)(2,1)} async-done(((bf16[512,2048]{1,0:T(8,128)(2,1)}), bf16[512,2048]{1,0:T(8,128)(2,1)}) %all-reduce.3.cloned.1.call-update) | async-done | bytes 2097168 | tf_op jit(solution)/shard_map/psum | solution.py:68
  311.2 3.1 multiply_reduce_fusion
  314.7 1.2 fusion.5
  316.0 3.7 collective-permute-start
  319.7 1.1 fusion.106
  321.2 5.2 %collective-permute-done = bf16[512,256]{0,1:T(8,128)(2,1)S(1)} collective-permute-done((bf16[512,256]{0,1:T(8,128)(2,1)S(1)}, bf16[512,256]{0,1:T(8,128)(2,1)S(1)}, u32[]{:S(2)}, u32[]{:S(2)}) %collective-permute-start) | collective-permute-done | bytes 262176 | tf_op jit(solution)/shard_map/ppermute | solution.py:28
  326.4 1.0 fusion.107
  327.4 1.9 collective-permute-start.1
  329.7 8.1 %collective-permute-done.1 = bf16[512,256]{0,1:T(8,128)(2,1)S(1)} collective-permute-done((bf16[512,256]{0,1:T(8,128)(2,1)S(1)}, bf16[512,256]{0,1:T(8,128)(2,1)S(1)}, u32[]{:S(2)}, u32[]{:S(2)}) %collective-permute-start.1) | collective-permute-done | bytes 262176 | tf_op jit(solution)/shard_map/ppermute | solution.py:28
  337.8 1.0 fusion.105
  338.8 1.9 collective-permute-start.2
  341.1 8.1 %collective-permute-done.2 = bf16[512,256]{0,1:T(8,128)(2,1)S(1)} collective-permute-done((bf16[512,256]{0,1:T(8,128)(2,1)S(1)}, bf16[512,256]{0,1:T(8,128)(2,1)S(1)}, u32[]{:S(2)}, u32[]{:S(2)}) %collective-permute-start.2) | collective-permute-done | bytes 262176 | tf_op jit(solution)/shard_map/ppermute | solution.py:28
  349.2 1.0 fusion.104
  350.3 1.9 collective-permute-start.3
  352.5 8.1 %collective-permute-done.3 = bf16[512,256]{0,1:T(8,128)(2,1)S(1)} collective-permute-done((bf16[512,256]{0,1:T(8,128)(2,1)S(1)}, bf16[512,256]{0,1:T(8,128)(2,1)S(1)}, u32[]{:S(2)}, u32[]{:S(2)}) %collective-permute-start.3) | collective-permute-done | bytes 262176 | tf_op jit(solution)/shard_map/ppermute | solution.py:28
  360.7 2.0 fusion.103
  362.7 3.5 convolution_convert_fusion.1
  366.3 43.3 %reduce-scatter.2.cloned.1.call-done = bf16[128,1024]{1,0:T(8,128)(2,1)} async-done(((bf16[1024,1024]{1,0:T(8,128)(2,1)}), bf16[128,1024]{1,0:T(8,128)(2,1)}) %reduce-scatter.2.cloned.1.call-update) | async-done | bytes 262160 | tf_op jit(solution)/shard_map/reduce_scatter | solution.py:147
  (286 shorter events, 86.1 us)
Async XLA Ops:
  6.5 232.7 %copy-start = (bf16[1024,1024]{1,0:T(8,128)(2,1)S(1)}, bf16[1024,1024]{1,0:T(8,128)(2,1)}, u32[]{:S(2)}) copy-start(bf16[1024,1024]{1,0:T(8,128)(2,1)} %param.19) | copy-start | bytes 6291460
  6.5 219.2 %all-gather.4.cloned.1.call-start = ((), (), s32[]{:S(2)}) async-start(), calls=%async_computation.1 | async-start | bytes 3727360 | tf_op jit(solution)/shard_map/all_gather | solution.py:58
  7.3 218.5 %all-gather.6.cloned.1.call-start = ((), (), s32[]{:S(2)}) async-start(), calls=%async_computation.2 | async-start | bytes 3727360 | tf_op jit(solution)/shard_map/all_gather | solution.py:65
  8.0 303.2 %all-reduce.3.cloned.1.call-start = ((), (), s32[]{:S(2)}) async-start(), calls=%async_computation.3 | async-start | bytes 4194304 | tf_op jit(solution)/shard_map/psum | solution.py:68
  239.2 0.9 copy-start.4
  239.2 1.8 copy-start.5
  239.2 170.4 %reduce-scatter.2.cloned.1.call-start = ((), (), s32[]{:S(2)}) async-start(), calls=%async_computation.4 | async-start | bytes 2359296 | tf_op jit(solution)/shard_map/reduce_scatter | solution.py:147
  240.1 74.2 %copy-start.6 = (bf16[2048,256]{1,0:T(8,128)(2,1)S(1)}, bf16[2048,256]{1,0:T(8,128)(2,1)}, u32[]{:S(2)}) copy-start(bf16[2048,256]{1,0:T(8,128)(2,1)} %param.18) | copy-start | bytes 3145732
  311.2 3.1 copy-start.1
  311.2 3.5 copy-start.2
  316.0 10.4 %collective-permute-start = (bf16[512,256]{0,1:T(8,128)(2,1)S(1)}, bf16[512,256]{0,1:T(8,128)(2,1)S(1)}, u32[]{:S(2)}, u32[]{:S(2)}) collective-permute-start(bf16[512,256]{0,1:T(8,128)(2,1)S(1)} %bitcast.99), channel_id=1, source_target_pairs={{0,8},{8,16},{16,24},{24,32},{32,40},{40,48},{48,56},{56,64},{64,7... | collective-permute-start | bytes 786440 | tf_op jit(solution)/shard_map/ppermute | solution.py:28
  327.4 10.4 %collective-permute-start.1 = (bf16[512,256]{0,1:T(8,128)(2,1)S(1)}, bf16[512,256]{0,1:T(8,128)(2,1)S(1)}, u32[]{:S(2)}, u32[]{:S(2)}) collective-permute-start(bf16[512,256]{0,1:T(8,128)(2,1)S(1)} %collective-permute-done), channel_id=1, source_target_pairs={{0,8},{8,16},{16,24},{24,32},{32,40},{40,48},{48,56},{56,64},{64,7... | collective-permute-start | bytes 786440 | tf_op jit(solution)/shard_map/ppermute | solution.py:28
  338.8 10.4 %collective-permute-start.2 = (bf16[512,256]{0,1:T(8,128)(2,1)S(1)}, bf16[512,256]{0,1:T(8,128)(2,1)S(1)}, u32[]{:S(2)}, u32[]{:S(2)}) collective-permute-start(bf16[512,256]{0,1:T(8,128)(2,1)S(1)} %collective-permute-done.1), channel_id=1, source_target_pairs={{0,8},{8,16},{16,24},{24,32},{32,40},{40,48},{48,56},{56,64},{64,7... | collective-permute-start | bytes 786440 | tf_op jit(solution)/shard_map/ppermute | solution.py:28
  350.3 10.4 %collective-permute-start.3 = (bf16[512,256]{0,1:T(8,128)(2,1)S(1)}, bf16[512,256]{0,1:T(8,128)(2,1)S(1)}, u32[]{:S(2)}, u32[]{:S(2)}) collective-permute-start(bf16[512,256]{0,1:T(8,128)(2,1)S(1)} %collective-permute-done.2), channel_id=1, source_target_pairs={{0,8},{8,16},{16,24},{24,32},{32,40},{40,48},{48,56},{56,64},{64,7... | collective-permute-start | bytes 786440 | tf_op jit(solution)/shard_map/ppermute | solution.py:28
  360.7 2.0 copy-start.3
Sparse Core Ops, SparseCore 0:
  10.4 90.1 all-gather.3
  103.6 82.9 all-gather.5
  239.3 71.8 all-reduce.2
  366.4 43.1 reduce-scatter.1
where the time goes:
time: 418 us; the launch traced here: 416 us
  waiting for transfers between devices  145 us (35%)
  blocking collectives  72.3 us (17%)
  other arithmetic  62.3 us (15%)
  local copies, waits for them, and re-layouts  43 us (10%)
  loops' own time  41.1 us (10%)
  matrix products  26.5 us (6%)
  between operations  16.7 us (4%)
  starting transfers between devices  9.62 us (2%)
    psum x1, waiting for transfers between devices, on_device(): lax.psum(partial_value.astype(jnp.bfloat16), 'mp').astype(jnp.float32)  70.2 us
    all_gather x1, blocking collectives, entering(): pieces = jax.tree.map(lambda part: lax.all_gather(part, axis), value)  48.6 us
    reduce_scatter x1, waiting for transfers between devices, on_device(): lax.psum_scatter(jnp.dot(attended, out_weight, preferred_element_type=jnp...  43.3 us
    another operation x1, loops' own time, entering(): return lax.fori_loop(0, count - 1, step, so_far)  41.1 us
    dynamic_slice x63, local copies, waits for them, and re-layouts, step(): longer = join(so_far, jax.tree.map(lambda part: part[position], pieces))  39 us
    while x63, other arithmetic  38.5 us
    ppermute x4, waiting for transfers between devices, from_behind(): lax.ppermute(value, axis, [(source, source + steps) for source in range(l...  29.6 us
    unnamed x1, blocking collectives  23.7 us
  transfers between devices with their start and end apart: 8, of which 6 were waited for; matrix products, arithmetic and copies ran while one was open for 25% of the time, Pallas kernels for 0%

commit v1 on v0

--- a/solution.py
+++ b/solution.py
@@ -65,7 +65,9 @@
         lax.all_gather(down_weight, "seq", axis=1, tiled=True),
         preferred_element_type=jnp.float32,
     )
-    mixed_out = lax.psum(partial_value.astype(jnp.bfloat16), "mp").astype(jnp.float32)
+    mixed_out = jnp.sum(lax.all_gather(partial_value.astype(jnp.bfloat16), "mp"), axis=0).astype(
+        jnp.float32
+    )
     kv_in = scale_rows(patch_states.astype(jnp.float32) + mixed_out, kv_scale).astype(jnp.bfloat16)
     heads_here = kv_weight.shape[1] // (2 * HS)
     projected = jnp.dot(kv_in, kv_weight, preferred_element_type=jnp.float32).reshape(

time: 418 us -> 444 us (1.062)
  waiting for transfers between devices: 145 us -> 170 us
  other arithmetic: 62.3 us -> 69 us
  local copies, waits for them, and re-layouts: 43 us -> 38.3 us
    all_gather x1, waiting for transfers between devices: 0.02 us -> 85.8 us  [on_device(): lax.all_gather(down_weight, 'seq', axis=1, tiled=True)]
    psum x1 -> x0, waiting for transfers between devices: 70.2 us -> none  [on_device(): lax.psum(partial_value.astype(jnp.bfloat16), 'mp').astype(jnp.float32)]
    all_gather x1, waiting for transfers between devices: 0.02 us -> 13.5 us  [on_device(): lax.all_gather(up_weight, 'seq', axis=0, tiled=True)]
    reduce_sum x0 -> x1, other arithmetic: none -> 10.8 us  [on_device(): jnp.sum(lax.all_gather(partial_value.astype(jnp.bfloat16), 'mp'), axis=0)]
    unnamed x1, blocking collectives: 23.7 us -> 30.7 us
    all_gather x1, blocking collectives: 48.6 us -> 42 us  [entering(): pieces = jax.tree.map(lambda part: lax.all_gather(part, axis), value)]
    reduce_scatter x1, waiting for transfers between devices: 43.3 us -> 38.7 us  [on_device(): lax.psum_scatter(jnp.dot(attended, out_weight, preferred_element_type=jnp...]
  transfers between devices with their start and end apart: 8 -> 8, of which waited for: 6 -> 7; matrix products, arithmetic and copies ran while one was open for 25% -> 22% of each run, Pallas kernels for 0% -> 0%
where the time goes in v1:
time: 444 us; the launch traced here: 441 us
  waiting for transfers between devices  170 us (38%)
  blocking collectives  72.7 us (16%)
  other arithmetic  69 us (16%)
  local copies, waits for them, and re-layouts  38.3 us (9%)
  loops' own time  37.3 us (8%)
  matrix products  27.7 us (6%)
  between operations  16.6 us (4%)
  starting transfers between devices  8.67 us (2%)
    all_gather x1, waiting for transfers between devices, on_device(): lax.all_gather(down_weight, 'seq', axis=1, tiled=True)  85.8 us
    all_gather x1, blocking collectives, entering(): pieces = jax.tree.map(lambda part: lax.all_gather(part, axis), value)  42 us
    reduce_scatter x1, waiting for transfers between devices, on_device(): lax.psum_scatter(jnp.dot(attended, out_weight, preferred_element_type=jnp...  38.7 us
    another operation x1, loops' own time, entering(): return lax.fori_loop(0, count - 1, step, so_far)  37.3 us
    dynamic_slice x63, local copies, waits for them, and re-layouts, step(): longer = join(so_far, jax.tree.map(lambda part: part[position], pieces))  35.2 us
    while x63, other arithmetic  34.7 us
    ppermute x4, waiting for transfers between devices, from_behind(): lax.ppermute(value, axis, [(source, source + steps) for source in range(l...  30.9 us
    unnamed x1, blocking collectives  30.7 us
  transfers between devices with their start and end apart: 8, of which 7 were waited for; matrix products, arithmetic and copies ran while one was open for 22% of the time, Pallas kernels for 0%

profile of v1, /device:TPU:8, one launch (start us, length us, event | category | flops | bytes accessed | tf_op | source)
XLA Modules:
  0.0 440.6 jit_solution(13266938854479148277)
XLA Ops:
  6.5 0.7 all-gather.6.cloned.1.call-update
  7.3 0.7 all-gather.8.cloned.1.call-update
  8.1 0.7 convert_element_type.73
  8.8 0.7 convert_element_type.78
  10.1 1.3 dynamic-slice
  11.5 0.8 dynamic-update-slice
  12.3 30.7 %all-reduce = s32[64]{0:T(128)S(1)} all-reduce(s32[64]{0:T(128)S(1)} %dynamic-update-slice), channel_id=1, replica_groups=mesh['seq'=64,'mp'=8] {'seq'}, use_global_device_ids=true, to_apply=%add | all-reduce | flops 64 | bytes 512
  43.0 42.0 %all-gather.1 = s32[64,1,4]{2,1,0:T(1,128)S(1)} all-gather(s32[1,1,4]{2,1,0:T(1,128)S(1)} %fusion.71), channel_id=1, replica_groups=mesh['seq'=64,'mp'=8] {'seq'}, dimensions={0}, use_global_device_ids=true | all-gather | bytes 1040 | tf_op jit(solution)/shard_map/all_gather | solution.py:13
  85.0 2.1 fusion.2
  87.1 13.5 %all-gather.6.cloned.1.call-done = bf16[2048,896]{1,0:T(8,128)(2,1)} async-done(((bf16[32,896]{1,0:T(8,128)(2,1)}), bf16[2048,896]{1,0:T(8,128)(2,1)}) %all-gather.6.cloned.1.call-update) | async-done | bytes 3670032 | tf_op jit(solution)/shard_map/all_gather | solution.py:58
  100.6 85.8 %all-gather.8.cloned.1.call-done = bf16[896,2048]{0,1:T(8,128)(2,1)} async-done(((bf16[896,32]{0,1:T(8,128)(2,1)}), bf16[896,2048]{0,1:T(8,128)(2,1)}) %all-gather.8.cloned.1.call-update) | async-done | bytes 3670032 | tf_op jit(solution)/shard_map/all_gather | solution.py:65
  186.4 13.4 %convolution_convert_fusion = bf16[512,2048]{1,0:T(8,128)(2,1)} fusion(bf16[896,2048]{0,1:T(8,128)(2,1)} %all-gather.8.cloned.1.call-done, bf16[2048,896]{1,0:T(8,128)(2,1)} %all-gather.6.cloned.1.call-done, bf16[512,2048]{1,0:T(8,128)(2,1)} %param.13, f32[2048]{0:T(1024)S(1)} %convert_element_type.73, f32[512]{0:T(512)S(1)} %add_rsqrt_fusion.3), kind=kOutput, calls=%fused_computation.15 | convolution fusion | flops 3793158144 | bytes 11544576 | tf_op jit(solution)/shard_map/dot_general | solution.py:63
  200.0 119.4 %while.15 = (s32[]{:T(128)}, s32[4]{0:T(128)S(1)}, s32[]{:T(128)}, s32[64]{0:T(128)S(1)}, s32[64,4]{1,0:T(8,128)S(1)}, /*index=5*/s32[]{:T(128)}, s32[]{:T(128)}, s32[]{:T(128)}) while((s32[]{:T(128)}, s32[4]{0:T(128)S(1)}, s32[]{:T(128)}, s32[64]{0:T(128)S(1)}, s32[64,4]{1,0:T(8,128)S(1)}, /*index=5*/s32[]{:T(128)}, ...), condition=%wide.region_7.8_spmd.clone.clone, body=%wide.region_5.7_spmd.clone.clone.sunk | while | flops 69 | bytes 301 | solution.py:22
  200.0 0.6 dynamic_slice.22
  201.9 0.6 dynamic_slice.22
  203.8 0.6 dynamic_slice.22
  205.7 0.6 dynamic_slice.22
  213.3 0.6 dynamic_slice.22
  236.1 0.6 dynamic_slice.22
  258.8 0.6 dynamic_slice.22
  275.8 0.6 dynamic_slice.22
  300.5 0.6 dynamic_slice.22
  319.4 0.6 reduce_sum.144
  320.1 0.6 fusion.102
  321.9 0.7 slice_reduce_fusion
  323.3 0.7 slice_reduce_fusion.1
  324.6 0.6 iota_compare_fusion.6
  325.2 0.6 iota_compare_fusion.3
  325.8 0.6 iota_compare_fusion.4
  327.1 0.8 multiply_reduce_fusion.1
  328.1 10.8 %reduce_sum.138 = bf16[512,2048]{1,0:T(8,128)(2,1)} reduce(bf16[8,512,2048]{2,1,0:T(8,128)(2,1)} %bitcast.98, bf16[]{:T(256)} %constant.113.clone.1), dimensions={0}, to_apply=%region_1.0 | reduce | flops 7340032 | bytes 18874370 | tf_op jit(solution)/shard_map/reduce_sum | solution.py:68
  338.9 3.1 multiply_reduce_fusion
  342.4 2.4 fusion.5
  344.9 2.6 collective-permute-start
  347.5 1.1 fusion.106
  348.9 6.3 %collective-permute-done = bf16[512,256]{0,1:T(8,128)(2,1)S(1)} collective-permute-done((bf16[512,256]{0,1:T(8,128)(2,1)S(1)}, bf16[512,256]{0,1:T(8,128)(2,1)S(1)}, u32[]{:S(2)}, u32[]{:S(2)}) %collective-permute-start) | collective-permute-done | bytes 262176 | tf_op jit(solution)/shard_map/ppermute | solution.py:28
  355.3 1.0 fusion.107
  356.3 1.9 collective-permute-start.1
  358.6 8.1 %collective-permute-done.1 = bf16[512,256]{0,1:T(8,128)(2,1)S(1)} collective-permute-done((bf16[512,256]{0,1:T(8,128)(2,1)S(1)}, bf16[512,256]{0,1:T(8,128)(2,1)S(1)}, u32[]{:S(2)}, u32[]{:S(2)}) %collective-permute-start.1) | collective-permute-done | bytes 262176 | tf_op jit(solution)/shard_map/ppermute | solution.py:28
  366.7 1.0 fusion.105
  367.7 1.9 collective-permute-start.2
  370.0 8.3 %collective-permute-done.2 = bf16[512,256]{0,1:T(8,128)(2,1)S(1)} collective-permute-done((bf16[512,256]{0,1:T(8,128)(2,1)S(1)}, bf16[512,256]{0,1:T(8,128)(2,1)S(1)}, u32[]{:S(2)}, u32[]{:S(2)}) %collective-permute-start.2) | collective-permute-done | bytes 262176 | tf_op jit(solution)/shard_map/ppermute | solution.py:28
  378.3 1.0 fusion.104
  379.3 1.9 collective-permute-start.3
  381.6 8.1 %collective-permute-done.3 = bf16[512,256]{0,1:T(8,128)(2,1)S(1)} collective-permute-done((bf16[512,256]{0,1:T(8,128)(2,1)S(1)}, bf16[512,256]{0,1:T(8,128)(2,1)S(1)}, u32[]{:S(2)}, u32[]{:S(2)}) %collective-permute-start.3) | collective-permute-done | bytes 262176 | tf_op jit(solution)/shard_map/ppermute | solution.py:28
  389.7 2.0 fusion.103
  391.7 3.6 convolution_convert_fusion.1
  395.3 38.7 %reduce-scatter.2.cloned.1.call-done = bf16[128,1024]{1,0:T(8,128)(2,1)} async-done(((bf16[1024,1024]{1,0:T(8,128)(2,1)}), bf16[128,1024]{1,0:T(8,128)(2,1)}) %reduce-scatter.2.cloned.1.call-update) | async-done | bytes 262160 | tf_op jit(solution)/shard_map/reduce_scatter | solution.py:149
  (285 shorter events, 79.8 us)
Async XLA Ops:
  6.5 320.6 %copy-start = (bf16[1024,1024]{1,0:T(8,128)(2,1)S(1)}, bf16[1024,1024]{1,0:T(8,128)(2,1)}, u32[]{:S(2)}) copy-start(bf16[1024,1024]{1,0:T(8,128)(2,1)} %param.19) | copy-start | bytes 6291460
  6.5 94.1 %all-gather.6.cloned.1.call-start = ((), (), s32[]{:S(2)}) async-start(), calls=%async_computation.1 | async-start | bytes 3727360 | tf_op jit(solution)/shard_map/all_gather | solution.py:58
  7.3 179.1 %all-gather.8.cloned.1.call-start = ((), (), s32[]{:S(2)}) async-start(), calls=%async_computation.2 | async-start | bytes 3727360 | tf_op jit(solution)/shard_map/all_gather | solution.py:65
  8.0 320.1 %all-gather.10.cloned.1.call-start = ((), (), s32[]{:S(2)}) async-start(), calls=%async_computation.4 | async-start | bytes 18874368 | tf_op jit(solution)/shard_map/all_gather | solution.py:68
  199.8 127.3 %copy-start.4 = (bf16[1024,128]{1,0:T(8,128)(2,1)S(1)}, bf16[1024,128]{1,0:T(8,128)(2,1)}, u32[]{:S(2)}) copy-start(bf16[1024,128]{1,0:T(8,128)(2,1)} %param.20) | copy-start | bytes 786436
  199.8 128.2 %copy-start.5 = (s32[1024]{0:T(1024)S(1)}, s32[1024]{0:T(1024)}, u32[]{:S(2)}) copy-start(s32[1024]{0:T(1024)} %param.23) | copy-start | bytes 12292
  199.8 234.2 %reduce-scatter.2.cloned.1.call-start = ((), (), s32[]{:S(2)}) async-start(), calls=%async_computation.3 | async-start | bytes 2359296 | tf_op jit(solution)/shard_map/reduce_scatter | solution.py:149
  338.9 3.1 copy-start.1
  338.9 3.5 copy-start.2
  344.9 10.4 %collective-permute-start = (bf16[512,256]{0,1:T(8,128)(2,1)S(1)}, bf16[512,256]{0,1:T(8,128)(2,1)S(1)}, u32[]{:S(2)}, u32[]{:S(2)}) collective-permute-start(bf16[512,256]{0,1:T(8,128)(2,1)S(1)} %bitcast.101), channel_id=1, source_target_pairs={{0,8},{8,16},{16,24},{24,32},{32,40},{40,48},{48,56},{56,64},{64,7... | collective-permute-start | bytes 786440 | tf_op jit(solution)/shard_map/ppermute | solution.py:28
  356.3 10.4 %collective-permute-start.1 = (bf16[512,256]{0,1:T(8,128)(2,1)S(1)}, bf16[512,256]{0,1:T(8,128)(2,1)S(1)}, u32[]{:S(2)}, u32[]{:S(2)}) collective-permute-start(bf16[512,256]{0,1:T(8,128)(2,1)S(1)} %collective-permute-done), channel_id=1, source_target_pairs={{0,8},{8,16},{16,24},{24,32},{32,40},{40,48},{48,56},{56,64},{64,7... | collective-permute-start | bytes 786440 | tf_op jit(solution)/shard_map/ppermute | solution.py:28
  367.7 10.5 %collective-permute-start.2 = (bf16[512,256]{0,1:T(8,128)(2,1)S(1)}, bf16[512,256]{0,1:T(8,128)(2,1)S(1)}, u32[]{:S(2)}, u32[]{:S(2)}) collective-permute-start(bf16[512,256]{0,1:T(8,128)(2,1)S(1)} %collective-permute-done.1), channel_id=1, source_target_pairs={{0,8},{8,16},{16,24},{24,32},{32,40},{40,48},{48,56},{56,64},{64,7... | collective-permute-start | bytes 786440 | tf_op jit(solution)/shard_map/ppermute | solution.py:28
  379.3 10.4 %collective-permute-start.3 = (bf16[512,256]{0,1:T(8,128)(2,1)S(1)}, bf16[512,256]{0,1:T(8,128)(2,1)S(1)}, u32[]{:S(2)}, u32[]{:S(2)}) collective-permute-start(bf16[512,256]{0,1:T(8,128)(2,1)S(1)} %collective-permute-done.2), channel_id=1, source_target_pairs={{0,8},{8,16},{16,24},{24,32},{32,40},{40,48},{48,56},{56,64},{64,7... | collective-permute-start | bytes 786440 | tf_op jit(solution)/shard_map/ppermute | solution.py:28
  389.7 2.0 copy-start.3
Sparse Core Ops, SparseCore 0:
  10.4 90.1 all-gather.5
  103.6 82.6 all-gather.7
  199.9 87.3 all-gather.9
  395.4 38.5 reduce-scatter.1
